TPU v7x, 512 devices: a whole 4x4x16 slice. The times are simulated.
512 devices in a mesh: seq: 32 (over z, core), hid: 16 (over x, y).
Axes of the slice: x: 4, y: 4, z: 16, core: 2. Of those that a mesh axis runs over, the one named last changes fastest.
Arguments:
- activations: bfloat16 [16384, 4096], P('seq'), may hold values from -6 to 6
- w_inner: bfloat16 [4096, 4096], P('seq', 'hid'), may hold values from -0.09375 to 0.09375
- w_gate: bfloat16 [4096, 4096], P('seq', 'hid'), may hold values from -0.09375 to 0.09375
- w_groups: bfloat16 [4096, 1024], P('seq'), may hold values from -0.09375 to 0.09375
- w_step: bfloat16 [4096, 64], P('seq'), may hold values from -0.09375 to 0.09375
- w_out: bfloat16 [4096, 4096], P('seq', 'hid'), may hold values from -0.09375 to 0.09375
- conv_inner: float32 [4, 4096], P(None, 'hid'), may hold values from -3 to 3
- conv_groups: float32 [4, 1024], replicated, may hold values from -3 to 3
- step_bias: float32 [64], P('hid'), may hold values from -4 to 0
- decay_log: float32 [64], P('hid'), may hold values from -9 to -1
- skip_gain: float32 [64], P('hid'), may hold values from 0.5 to 1.5
- norm_gain: float32 [4096], P('hid'), may hold values from 0.5 to 1.5
Outputs:
- layer_out: bfloat16 [16384, 4096], P('seq', 'hid')
All inputs are finite; a program needn't handle non-finite values.
Results may differ from a plain program's by a relative error of at most 0.02.
Values may be sent and summed in bfloat16 or wider, within the bound.
A program may use at most 64 MiB of HBM per device.

v0:
```python
import jax
import jax.numpy as jnp
from jax import lax
from jax.sharding import PartitionSpec as P

HEADS = 64
P_SIZE = 64
N = 128
G = 4
Q = 256
K = 4
INNER = 4096


def from_behind(block, axis, distance):
    devices = range(lax.axis_size(axis))
    route = [(i - distance, i) for i in devices if i - distance in devices]
    return lax.ppermute(block, axis, route)


def carried_in(array, axis, join, neutral):
    place = lax.axis_index(axis)
    gathered = jax.tree.map(
        lambda a, kind: lax.all_gather(a.astype(kind), axis), array, (jnp.bfloat16, jnp.bfloat16)
    )
    state = jax.tree.map(lambda a, e: jnp.zeros_like(a) + jnp.asarray(e, a.dtype), array, neutral)

    def one(step, state):
        return join(
            state,
            jax.tree.map(
                lambda a, own: lax.dynamic_index_in_dim(a, step, 0, False).astype(own.dtype),
                gathered,
                array,
            ),
        )

    return lax.fori_loop(0, place, one, state)


def causal_conv(values, before, kernel):
    length = values.shape[0]
    extended = jnp.concatenate([before, values], axis=0)
    summed = jnp.zeros(values.shape, jnp.float32)
    for position in range(kernel.shape[0]):
        summed = (
            summed + extended[position : position + length].astype(jnp.float32) * kernel[position]
        )
    return jax.nn.silu(summed).astype(jnp.bfloat16)


def combine_states(earlier, later):
    return (earlier[0] * later[0], later[0][:, None, None] * earlier[1] + later[1])


def roll_state(state, inputs):
    total_here, fresh_here = inputs
    return (jnp.exp(total_here)[:, None, None] * state + fresh_here, state)


def local(
    activations,
    w_inner,
    w_gate,
    w_groups,
    w_step,
    w_out,
    conv_inner,
    conv_groups,
    step_bias,
    decay_log,
    skip_gain,
    norm_gain,
):
    tok_rows = activations.shape[0]
    heads_dev = step_bias.shape[0]
    width_dev = w_inner.shape[1]
    head_block = lax.axis_index("hid")
    group_cols = 2 * N
    group_index = head_block * heads_dev // (HEADS // G)
    step_cols = lax.dynamic_slice_in_dim(w_step, head_block * heads_dev, heads_dev, 1)
    own_cols = lax.dynamic_slice_in_dim(w_groups, group_index * group_cols, group_cols, 1)
    piece_inner = lax.all_gather(w_inner, "seq", axis=0, tiled=True)
    piece_gate = lax.all_gather(w_gate, "seq", axis=0, tiled=True)
    piece_groups = lax.all_gather(own_cols, "seq", axis=0, tiled=True)
    piece_step = lax.all_gather(step_cols, "seq", axis=0, tiled=True)
    piece_out = lax.all_gather(w_out, "seq", axis=0, tiled=True)
    acc_inner = jnp.dot(activations, piece_inner, preferred_element_type=jnp.float32)
    acc_gate = jnp.dot(activations, piece_gate, preferred_element_type=jnp.float32)
    acc_groups = jnp.dot(activations, piece_groups, preferred_element_type=jnp.float32)
    acc_step = jnp.dot(activations, piece_step, preferred_element_type=jnp.float32)
    groups_in = acc_groups.astype(jnp.bfloat16)
    inner_in = acc_inner.astype(jnp.bfloat16)
    gate_in = acc_gate.astype(jnp.bfloat16)
    conv_group = lax.dynamic_slice_in_dim(conv_groups, group_index * group_cols, group_cols, 1)
    tail_rows = K - 1
    inner_prev, groups_prev = from_behind(
        (inner_in[tok_rows - tail_rows :], groups_in[tok_rows - tail_rows :]), "seq", 1
    )
    inner_conv = causal_conv(inner_in, inner_prev, conv_inner)
    groups_conv = causal_conv(groups_in, groups_prev, conv_group)
    step_size = jax.nn.softplus(acc_step + step_bias)
    rates = -jnp.exp(decay_log)
    span_count = tok_rows // Q
    heads_x = inner_conv.reshape(span_count, Q, heads_dev, P_SIZE)
    b_in = groups_conv[:, :N].reshape(span_count, Q, N)
    c_out = groups_conv[:, N:].reshape(span_count, Q, N)
    block_dt = step_size.reshape(span_count, Q, heads_dev)
    cum_decay = jnp.cumsum(block_dt * rates, axis=1)
    scores = jnp.einsum("ctn,csn->cts", c_out, b_in, preferred_element_type=jnp.float32)
    ahead = jnp.arange(Q)[:, None] >= jnp.arange(Q)[None, :]
    decay_t = jnp.swapaxes(cum_decay, 1, 2)
    gap = jnp.where(ahead, decay_t[:, :, :, None] - decay_t[:, :, None, :], -1e30)
    mixing = (scores[:, None] * jnp.exp(gap) * jnp.swapaxes(block_dt, 1, 2)[:, :, None, :]).astype(
        jnp.bfloat16
    )
    intra = jnp.einsum("chts,cshp->cthp", mixing, heads_x, preferred_element_type=jnp.float32)
    span_total = cum_decay[:, -1]
    weights_in = jnp.exp(span_total[:, None, :] - cum_decay) * block_dt
    weighted = (b_in[:, :, None, :] * weights_in[:, :, :, None]).astype(jnp.bfloat16)
    fresh = jnp.einsum("cshn,cshp->chnp", weighted, heads_x, preferred_element_type=jnp.float32)
    zero_state = jnp.zeros((heads_dev, N, P_SIZE), jnp.float32)
    local_end, starts = lax.scan(roll_state, zero_state, (span_total, fresh))
    log_total = jnp.sum(span_total, axis=0)
    prior = jnp.cumsum(span_total, axis=0) - span_total
    identity = (jnp.ones((heads_dev,), jnp.float32), zero_state)
    state_in = carried_in((jnp.exp(log_total), local_end), "seq", combine_states, identity)[1]
    span_in = starts + jnp.exp(prior)[:, :, None, None] * state_in[None]
    inter = jnp.einsum(
        "ctn,chnp->cthp", c_out.astype(jnp.float32), span_in, precision=lax.Precision.HIGHEST
    )
    inter = inter * jnp.exp(cum_decay)[:, :, :, None]
    mixed = (intra + inter).reshape(tok_rows, width_dev) + jnp.repeat(
        skip_gain, P_SIZE
    ) * inner_conv.astype(jnp.float32)
    gated = mixed * jax.nn.silu(gate_in.astype(jnp.float32))
    squares = lax.psum(jnp.sum(gated * gated, axis=1), "hid")
    normed = (gated * lax.rsqrt(squares / INNER + 1e-05)[:, None] * norm_gain).astype(jnp.bfloat16)
    terms = lax.dot_general(
        normed, piece_out, (((1,), (1,)), ((), ())), preferred_element_type=jnp.float32
    )
    return lax.psum_scatter(terms.astype(jnp.bfloat16), "hid", scatter_dimension=1, tiled=True)


def solution(mesh):
    in_specs = (
        P("seq", None),
        P("seq", "hid"),
        P("seq", "hid"),
        P("seq", None),
        P("seq", None),
        P("seq", "hid"),
        P(None, "hid"),
        P(),
        P("hid"),
        P("hid"),
        P("hid"),
        P("hid"),
    )
    out_specs = P("seq", "hid")
    return jax.shard_map(local, mesh=mesh, in_specs=in_specs, out_specs=out_specs, check_vma=False)
```

profile of v0, /device:TPU:32, one launch (start us, length us, event | category | flops | bytes accessed | tf_op | source)
XLA Modules:
  0.0 480.8 jit_solution(4946631433308588536)
XLA Ops:
  6.5 0.9 copy-done
  7.5 0.6 constant_dynamic-slice_fusion.4
  8.2 0.7 all-gather.8.cloned.1.call-update
  9.0 0.7 constant_dynamic-slice_fusion.3
  9.7 34.2 %all_gather.27 = bf16[4096,4]{0,1:T(4,128)(2,1)S(1)} all-gather(bf16[128,4]{0,1:T(4,128)(2,1)S(1)} %constant_dynamic-slice_fusion.3), channel_id=1, replica_groups=mesh['seq'=32,'hid'=16] {'seq'}, dimensions={0}, use_global_device_ids=true | all-gather | bytes 33792 | tf_op jit(solution)/shard_map/all_gather | solution.py:86
  43.8 0.7 exponential_negate_fusion
  44.5 3.5 compare_select_fusion
  48.1 2.4 reduce-window.6
  50.9 0.9 constant_dynamic-slice_fusion.2
  52.1 32.9 %all-gather.10.cloned.1.call-done = bf16[4096,256]{1,0:T(8,128)(2,1)} async-done(((bf16[128,256]{1,0:T(8,128)(2,1)}), bf16[4096,256]{1,0:T(8,128)(2,1)}) %all-gather.10.cloned.1.call-update) | async-done | bytes 2097168 | tf_op jit(solution)/shard_map/all_gather | solution.py:85
  85.0 4.1 fusion.4
  89.2 2.1 collective-permute-start.1
  91.3 64.3 %all-gather.8.cloned.1.call-done = bf16[4096,256]{1,0:T(8,128)(2,1)} async-done(((bf16[128,256]{1,0:T(8,128)(2,1)}), bf16[4096,256]{1,0:T(8,128)(2,1)}) %all-gather.8.cloned.1.call-update) | async-done | bytes 2097168 | tf_op jit(solution)/shard_map/all_gather | solution.py:83
  155.6 4.1 convolution_convert_fusion.3
  159.8 2.1 collective-permute-start
  162.3 2.3 collective-permute-done
  165.5 0.8 fusion.12
  166.7 0.7 copy.84
  168.7 1.3 dynamic-slice
  170.9 44.1 %all-reduce = bf16[128]{0:T(256)(128)(2,1)S(1)} all-reduce(bf16[128]{0:T(256)(128)(2,1)S(1)} %dynamic-update-slice), channel_id=2, replica_groups=mesh['seq'=32,'hid'=16] {'seq'}, use_global_device_ids=true, to_apply=%add | all-reduce | flops 128 | bytes 512
  215.5 21.5 %all-gather.16.cloned.1.call-done = bf16[128,128,64]{1,2,0:T(8,128)(2,1)} async-done(((bf16[4,128,64]{1,2,0:T(8,128)(2,1)}), bf16[128,128,64]{1,2,0:T(8,128)(2,1)}) %all-gather.16.cloned.1.call-update) | async-done | bytes 2097168 | tf_op jit(solution)/shard_map/all_gather | solution.py:24
  237.1 2.3 while.25
  237.1 0.9 constant_dynamic-slice_fusion.6
  238.2 0.9 constant_dynamic-slice_fusion.6
  240.1 0.8 fusion.2
  241.2 0.6 reshape.121
  241.8 65.7 %all-gather.12.cloned.1.call-done = bf16[4096,256]{1,0:T(8,128)(2,1)} async-done(((bf16[128,256]{1,0:T(8,128)(2,1)}), bf16[4096,256]{1,0:T(8,128)(2,1)}) %all-gather.12.cloned.1.call-update) | async-done | bytes 2097168 | tf_op jit(solution)/shard_map/all_gather | solution.py:84
  307.5 4.3 multiply_reduce_fusion
  311.8 40.3 %psum.7 = f32[512]{0:T(512)S(1)} all-reduce(f32[512]{0:T(512)S(1)} %get-tuple-element.172), channel_id=1, replica_groups=mesh['seq'=32,'hid'=16] {'hid'}, use_global_device_ids=true, to_apply=%region_9.10 | all-reduce | flops 512 | bytes 4096 | tf_op jit(solution)/shard_map/psum | solution.py:137
  352.1 25.9 %all-gather.14.cloned.1.call-done = bf16[4096,256]{1,0:T(8,128)(2,1)} async-done(((bf16[128,256]{1,0:T(8,128)(2,1)}), bf16[4096,256]{1,0:T(8,128)(2,1)}) %all-gather.14.cloned.1.call-update) | async-done | bytes 2097168 | tf_op jit(solution)/shard_map/all_gather | solution.py:87
  378.0 4.8 %convolution_convert_fusion = bf16[512,4096]{1,0:T(8,128)(2,1)} fusion(bf16[4096,256]{1,0:T(8,128)(2,1)} %all-gather.14.cloned.1.call-done, f32[512,256]{1,0:T(8,128)S(1)} %get-tuple-element.173, f32[256]{0:T(256)S(1)} %copy-done.1, f32[512]{0:T(512)S(1)} %add_rsqrt_fusion), kind=kOutput, calls=%fused_computation.8 | convolution fusion | flops 1076232192 | bytes 6818816 | tf_op jit(solution)/shard_map/dot_general | solution.py:139
  382.9 91.1 %reduce-scatter.2.cloned.1.call-done = bf16[512,256]{1,0:T(8,128)(2,1)} async-done(((bf16[512,4096]{1,0:T(8,128)(2,1)}), bf16[512,256]{1,0:T(8,128)(2,1)}) %reduce-scatter.2.cloned.1.call-update) | async-done | bytes 262160 | tf_op jit(solution)/shard_map/reduce_scatter | solution.py:142
  (70 shorter events, 6.4 us)
Async XLA Ops:
  6.5 1.0 copy-start
  6.5 78.5 %all-gather.10.cloned.1.call-start = ((), (), s32[]{:S(2)}) async-start(), calls=%async_computation.2 | async-start | bytes 2162688 | tf_op jit(solution)/shard_map/all_gather | solution.py:85
  8.1 147.5 %all-gather.8.cloned.1.call-start = ((), (), s32[]{:S(2)}) async-start(), calls=%async_computation.1 | async-start | bytes 2162688 | tf_op jit(solution)/shard_map/all_gather | solution.py:83
  8.9 228.1 %all-gather.16.cloned.1.call-start = ((), (), s32[]{:S(2)}) async-start(), calls=%async_computation.6 | async-start | bytes 2162688 | tf_op jit(solution)/shard_map/all_gather | solution.py:24
  44.5 7.5 %copy-start.2 = (f32[4,256]{1,0:T(4,128)S(1)}, f32[4,256]{1,0:T(4,128)}, u32[]{:S(2)}) copy-start(f32[4,256]{1,0:T(4,128)} %param.22) | copy-start | bytes 12292
  89.2 72.7 %collective-permute-start.1 = (bf16[3,256]{1,0:T(4,128)(2,1)S(1)}, bf16[3,256]{1,0:T(4,128)(2,1)S(1)}, u32[]{:S(2)}, u32[]{:S(2)}) collective-permute-start(bf16[3,256]{1,0:T(4,128)(2,1)S(1)} %slice.89), channel_id=1, source_target_pairs={{0,16},{16,32},{32,48},{48,64},{64,80},{80,96},{96,112},{112,128},... | collective-permute-start | bytes 4616 | tf_op jit(solution)/shard_map/ppermute | solution.py:18
  159.8 4.9 %collective-permute-start = (bf16[3,256]{1,0:T(4,128)(2,1)S(1)}, bf16[3,256]{1,0:T(4,128)(2,1)S(1)}, u32[]{:S(2)}, u32[]{:S(2)}) collective-permute-start(bf16[3,256]{1,0:T(4,128)(2,1)S(1)} %slice.84), channel_id=1, source_target_pairs={{0,16},{16,32},{32,48},{48,64},{64,80},{80,96},{96,112},{112,128},... | collective-permute-start | bytes 4616 | tf_op jit(solution)/shard_map/ppermute | solution.py:18
  166.3 48.7 %copy-start.3 = (f32[4]{0:T(128)S(1)}, f32[4]{0:T(128)}, u32[]{:S(2)}) copy-start(f32[4]{0:T(128)} %param.26) | copy-start | bytes 52
  167.4 140.1 %all-gather.12.cloned.1.call-start = ((), (), s32[]{:S(2)}) async-start(), calls=%async_computation.3 | async-start | bytes 2162688 | tf_op jit(solution)/shard_map/all_gather | solution.py:84
  168.0 210.0 %all-gather.14.cloned.1.call-start = ((), (), s32[]{:S(2)}) async-start(), calls=%async_computation.4 | async-start | bytes 2162688 | tf_op jit(solution)/shard_map/all_gather | solution.py:87
  168.6 305.3 %reduce-scatter.2.cloned.1.call-start = ((), (), s32[]{:S(2)}) async-start(), calls=%async_computation.5 | async-start | bytes 4456448 | tf_op jit(solution)/shard_map/reduce_scatter | solution.py:142
  241.8 136.2 %copy-start.1 = (f32[256]{0:T(256)S(1)}, f32[256]{0:T(256)}, u32[]{:S(2)}) copy-start(f32[256]{0:T(256)} %param.27) | copy-start | bytes 3076
Sparse Core Ops, SparseCore 0:
  9.5 75.5 all-gather.9
  87.1 68.4 all-gather.7
  167.5 69.4 all-gather.15
  239.0 68.4 all-gather.11
  309.5 68.4 all-gather.13
  383.0 90.8 reduce-scatter.1
where the time goes:
time: 483 us; the launch traced here: 481 us
  waiting for transfers between devices  306 us (63%)
  blocking collectives  119 us (25%)
  matrix products  22.9 us (5%)
  between operations  14.4 us (3%)
  local copies, waits for them, and re-layouts  9.82 us (2%)
  other arithmetic  4.96 us (1%)
    reduce_scatter x1, waiting for transfers between devices, local(): lax.psum_scatter(terms.astype(jnp.bfloat16), 'hid', scatter_dimension=1,...  91.1 us
    all_gather x1, waiting for transfers between devices, local(): piece_gate = lax.all_gather(w_gate, 'seq', axis=0, tiled=True)  65.7 us
    all_gather x1, waiting for transfers between devices, local(): piece_inner = lax.all_gather(w_inner, 'seq', axis=0, tiled=True)  64.3 us
    unnamed x1, blocking collectives  44.1 us
    psum x1, blocking collectives, local(): squares = lax.psum(jnp.sum(gated * gated, axis=1), 'hid')  40.3 us
    all_gather x1, blocking collectives, local(): piece_step = lax.all_gather(step_cols, 'seq', axis=0, tiled=True)  34.2 us
    all_gather x1, waiting for transfers between devices, local(): piece_groups = lax.all_gather(own_cols, 'seq', axis=0, tiled=True)  32.9 us
    all_gather x1, waiting for transfers between devices, local(): piece_out = lax.all_gather(w_out, 'seq', axis=0, tiled=True)  25.9 us
  transfers between devices with their start and end apart: 8, of which 7 were waited for; matrix products, arithmetic and copies ran while one was open for 6% of the time, Pallas kernels for 0%

commit v1 on v0

--- a/solution.py
+++ b/solution.py
@@ -84,7 +84,9 @@
     piece_gate = lax.all_gather(w_gate, "seq", axis=0, tiled=True)
     piece_groups = lax.all_gather(own_cols, "seq", axis=0, tiled=True)
     piece_step = lax.all_gather(step_cols, "seq", axis=0, tiled=True)
-    piece_out = lax.all_gather(w_out, "seq", axis=0, tiled=True)
+    piece_out = jnp.concatenate(
+        lax.all_to_all(jnp.stack([w_out] * lax.axis_size("seq")), "seq", 0, 0), axis=0
+    )
     acc_inner = jnp.dot(activations, piece_inner, preferred_element_type=jnp.float32)
     acc_gate = jnp.dot(activations, piece_gate, preferred_element_type=jnp.float32)
     acc_groups = jnp.dot(activations, piece_groups, preferred_element_type=jnp.float32)

time: 483 us -> 505 us (1.046)
  blocking collectives: 119 us -> 210 us
  waiting for transfers between devices: 306 us -> 219 us
  starting transfers between devices: 4.46 us -> 14.3 us
    unnamed x1, blocking collectives: 44.1 us -> 136 us
    all_gather x1, waiting for transfers between devices: 65.7 us -> 16 us  [local(): piece_gate = lax.all_gather(w_gate, 'seq', axis=0, tiled=True)]
    all_gather x1 -> x0, waiting for transfers between devices: 25.9 us -> none  [local(): piece_out = lax.all_gather(w_out, 'seq', axis=0, tiled=True)]
    all_gather x1, waiting for transfers between devices: 21.5 us -> 0.01 us  [carried_in(): lax.all_gather(a.astype(kind), axis)]
    reduce_scatter x1, waiting for transfers between devices: 91.1 us -> 103 us  [local(): lax.psum_scatter(terms.astype(jnp.bfloat16), 'hid', scatter_dimension=1,...]
    all_to_all x0 -> x1, starting transfers between devices: none -> 9.83 us  [local(): lax.all_to_all(jnp.stack([w_out] * lax.axis_size('seq')), 'seq', 0, 0)]
  transfers between devices with their start and end apart: 8 -> 8, of which waited for: 7 -> 5; matrix products, arithmetic and copies ran while one was open for 6% -> 8% of each run, Pallas kernels for 0% -> 0%
where the time goes in v1:
time: 505 us; the launch traced here: 503 us
  waiting for transfers between devices  219 us (43%)
  blocking collectives  210 us (42%)
  matrix products  24.1 us (5%)
  starting transfers between devices  14.3 us (3%)
  between operations  14 us (3%)
  local copies, waits for them, and re-layouts  13.9 us (3%)
  other arithmetic  7.7 us (2%)
    unnamed x1, blocking collectives  136 us
    reduce_scatter x1, waiting for transfers between devices, local(): lax.psum_scatter(terms.astype(jnp.bfloat16), 'hid', scatter_dimension=1,...  103 us
    all_gather x1, waiting for transfers between devices, local(): piece_inner = lax.all_gather(w_inner, 'seq', axis=0, tiled=True)  64.3 us
    psum x1, blocking collectives, local(): squares = lax.psum(jnp.sum(gated * gated, axis=1), 'hid')  40.3 us
    all_gather x1, blocking collectives, local(): piece_step = lax.all_gather(step_cols, 'seq', axis=0, tiled=True)  34.2 us
    all_gather x1, waiting for transfers between devices, local(): piece_groups = lax.all_gather(own_cols, 'seq', axis=0, tiled=True)  32.4 us
    all_gather x1, waiting for transfers between devices, local(): piece_gate = lax.all_gather(w_gate, 'seq', axis=0, tiled=True)  16 us
  transfers between devices with their start and end apart: 8, of which 5 were waited for; matrix products, arithmetic and copies ran while one was open for 8% of the time, Pallas kernels for 0%

profile of v1, /device:TPU:32, one launch (start us, length us, event | category | flops | bytes accessed | tf_op | source)
XLA Modules:
  0.0 503.0 jit_solution(7831252039685737083)
XLA Ops:
  6.5 0.9 copy-done
  8.2 0.7 all-gather.7.cloned.1.call-update
  9.7 34.2 %all_gather.24 = bf16[4096,4]{0,1:T(4,128)(2,1)S(1)} all-gather(bf16[128,4]{0,1:T(4,128)(2,1)S(1)} %constant_dynamic-slice_fusion.3), channel_id=1, replica_groups=mesh['seq'=32,'hid'=16] {'seq'}, dimensions={0}, use_global_device_ids=true | all-gather | bytes 33792 | tf_op jit(solution)/shard_map/all_gather | solution.py:86
  44.5 3.5 compare_select_fusion
  48.1 2.4 reduce-window.6
  50.9 0.9 constant_dynamic-slice_fusion.2
  52.7 32.4 %all-gather.9.cloned.1.call-done = bf16[4096,256]{1,0:T(8,128)(2,1)} async-done(((bf16[128,256]{1,0:T(8,128)(2,1)}), bf16[4096,256]{1,0:T(8,128)(2,1)}) %all-gather.9.cloned.1.call-update) | async-done | bytes 2097168 | tf_op jit(solution)/shard_map/all_gather | solution.py:85
  85.0 4.1 fusion.4
  89.2 2.1 collective-permute-start.1
  91.3 64.3 %all-gather.7.cloned.1.call-done = bf16[4096,256]{1,0:T(8,128)(2,1)} async-done(((bf16[128,256]{1,0:T(8,128)(2,1)}), bf16[4096,256]{1,0:T(8,128)(2,1)}) %all-gather.7.cloned.1.call-update) | async-done | bytes 2097168 | tf_op jit(solution)/shard_map/all_gather | solution.py:83
  155.6 4.1 convolution_convert_fusion.3
  159.8 2.1 collective-permute-start
  162.3 2.3 collective-permute-done
  165.5 0.8 fusion.12
  166.7 0.8 copy.84
  167.6 1.6 stack.2
  169.1 9.8 %all-to-all-start = ((bf16[32,128,256]{2,1,0:T(8,128)(2,1)}), bf16[32,128,256]{2,1,0:T(8,128)(2,1)S(1)}, u32[]{:S(2)}, u32[]{:S(2)}) async-start(bf16[32,128,256]{2,1,0:T(8,128)(2,1)} %stack.2), calls=%async_computation | async-start | bytes 4194304 | tf_op jit(solution)/shard_map/all_to_all | solution.py:88
  180.3 1.3 dynamic-slice
  182.5 135.6 %all-reduce = bf16[128]{0:T(256)(128)(2,1)S(1)} all-reduce(bf16[128]{0:T(256)(128)(2,1)S(1)} %dynamic-update-slice), channel_id=2, replica_groups=mesh['seq'=32,'hid'=16] {'seq'}, use_global_device_ids=true, to_apply=%add | all-reduce | flops 128 | bytes 512
  319.4 1.0 fusion.24
  320.5 2.3 while.25
  320.5 0.9 constant_dynamic-slice_fusion.6
  321.7 0.9 constant_dynamic-slice_fusion.6
  322.8 1.2 multiply_add_fusion
  324.5 2.7 fusion.2
  327.2 1.4 copy.93
  328.6 1.4 reshape.127
  330.0 16.0 %all-gather.11.cloned.1.call-done = bf16[4096,256]{1,0:T(8,128)(2,1)} async-done(((bf16[128,256]{1,0:T(8,128)(2,1)}), bf16[4096,256]{1,0:T(8,128)(2,1)}) %all-gather.11.cloned.1.call-update) | async-done | bytes 2097168 | tf_op jit(solution)/shard_map/all_gather | solution.py:84
  346.0 4.3 multiply_reduce_fusion
  350.3 40.3 %psum.7 = f32[512]{0:T(512)S(1)} all-reduce(f32[512]{0:T(512)S(1)} %get-tuple-element.172), channel_id=1, replica_groups=mesh['seq'=32,'hid'=16] {'hid'}, use_global_device_ids=true, to_apply=%region_9.10 | all-reduce | flops 512 | bytes 4096 | tf_op jit(solution)/shard_map/psum | solution.py:139
  390.7 3.2 convolution_convert_fusion
  393.9 102.5 %reduce-scatter.2.cloned.1.call-done = bf16[512,256]{1,0:T(8,128)(2,1)} async-done(((bf16[512,4096]{1,0:T(8,128)(2,1)}), bf16[512,256]{1,0:T(8,128)(2,1)}) %reduce-scatter.2.cloned.1.call-update) | async-done | bytes 262160 | tf_op jit(solution)/shard_map/reduce_scatter | solution.py:144
  (78 shorter events, 9.3 us)
Async XLA Ops:
  6.5 1.0 copy-start
  6.5 78.5 %all-gather.9.cloned.1.call-start = ((), (), s32[]{:S(2)}) async-start(), calls=%async_computation.3 | async-start | bytes 2162688 | tf_op jit(solution)/shard_map/all_gather | solution.py:85
  8.1 147.5 %all-gather.7.cloned.1.call-start = ((), (), s32[]{:S(2)}) async-start(), calls=%async_computation.2 | async-start | bytes 2162688 | tf_op jit(solution)/shard_map/all_gather | solution.py:83
  8.9 311.6 %all-gather.13.cloned.1.call-start = ((), (), s32[]{:S(2)}) async-start(), calls=%async_computation.6 | async-start | bytes 2162688 | tf_op jit(solution)/shard_map/all_gather | solution.py:24
  44.5 7.5 %copy-start.5 = (f32[4,256]{1,0:T(4,128)S(1)}, f32[4,256]{1,0:T(4,128)}, u32[]{:S(2)}) copy-start(f32[4,256]{1,0:T(4,128)} %param.22) | copy-start | bytes 12292
  89.2 72.7 %collective-permute-start.1 = (bf16[3,256]{1,0:T(4,128)(2,1)S(1)}, bf16[3,256]{1,0:T(4,128)(2,1)S(1)}, u32[]{:S(2)}, u32[]{:S(2)}) collective-permute-start(bf16[3,256]{1,0:T(4,128)(2,1)S(1)} %slice.89), channel_id=1, source_target_pairs={{0,16},{16,32},{32,48},{48,64},{64,80},{80,96},{96,112},{112,128},... | collective-permute-start | bytes 4616 | tf_op jit(solution)/shard_map/ppermute | solution.py:18
  159.8 4.9 collective-permute-start
  165.0 4.1 copy-start.1
  166.3 1.2 copy-start.3
  166.7 2.5 copy-start.2
  169.1 10.5 %copy-start.7 = (f32[4]{0:T(128)S(1)}, f32[4]{0:T(128)}, u32[]{:S(2)}) copy-start(f32[4]{0:T(128)} %param.26) | copy-start | bytes 52
  169.1 221.5 %all-to-all-start = ((bf16[32,128,256]{2,1,0:T(8,128)(2,1)}), bf16[32,128,256]{2,1,0:T(8,128)(2,1)S(1)}, u32[]{:S(2)}, u32[]{:S(2)}) async-start(bf16[32,128,256]{2,1,0:T(8,128)(2,1)} %stack.2), calls=%async_computation | async-start | bytes 4194304 | tf_op jit(solution)/shard_map/all_to_all | solution.py:88
  179.0 167.0 %all-gather.11.cloned.1.call-start = ((), (), s32[]{:S(2)}) async-start(), calls=%async_computation.4 | async-start | bytes 2162688 | tf_op jit(solution)/shard_map/all_gather | solution.py:84
  179.6 316.9 %reduce-scatter.2.cloned.1.call-start = ((), (), s32[]{:S(2)}) async-start(), calls=%async_computation.5 | async-start | bytes 4456448 | tf_op jit(solution)/shard_map/reduce_scatter | solution.py:144
  327.2 18.8 %copy-start.6 = (f32[256]{0:T(256)S(1)}, f32[256]{0:T(256)}, u32[]{:S(2)}) copy-start(f32[256]{0:T(256)} %mul.255) | copy-start | bytes 3076
  330.0 60.6 %copy-start.4 = (f32[256]{0:T(256)S(1)}, f32[256]{0:T(256)}, u32[]{:S(2)}) copy-start(f32[256]{0:T(256)} %param.27) | copy-start | bytes 3076
Sparse Core Ops, SparseCore 0:
  9.5 75.5 all-gather.8
  87.1 68.4 all-gather.6
  167.7 97.8 all-gather.12
  267.5 78.4 all-gather.10
  394.0 102.3 reduce-scatter.1
